TPU v7x, 768 devices: a whole 4x8x12 slice. The times are simulated.
768 devices in a mesh: proj: 3 (over z_hi), space: 256 (over y, x, z_lo, core).
Axes of the slice: x: 4, y: 8, z: 12 (z_hi: 3, z_lo: 4; z = z_hi * 4 + z_lo), core: 2. Of those that a mesh axis runs over, the one named last changes fastest.
Arguments:
- design: float32 [512, 64, 384], P('space', None, 'proj'), may hold values from 0.02 to 0.98
- solid_mask: int32 [512, 64, 384], P('space', None, 'proj'), may hold values 0 or 1
- void_mask: int32 [512, 64, 384], P('space', None, 'proj'), may hold values 0 or 1
- load_mask: int32 [512, 64, 384], P('space'), may hold values 0 or 1
- support_mask: int32 [512, 64, 384], P('space'), may hold values 0 or 1
- thresholds: int32 [3], P('proj'), may hold values from 300 to 700
- group_weight: float32 [3], P('proj'), may hold values from 0.5 to 2
Outputs:
- sensitivity: float32 [512, 64, 384], P('space', None, 'proj')
All inputs are finite; a program needn't handle non-finite values. No bound on the sum of `solid_mask` or of `void_mask` or of `load_mask` or of `support_mask` on one device may be relied on, other than what follows from the above.
Results may differ from a plain program's by a relative error of at most 0.0001.
Values sent between devices are 32-bit elements; how exact they have to be, the bound alone decides.
A program may use at most 32 MiB of HBM per device.

v0:
```python
import math

import jax
import jax.numpy as jnp
from jax import lax
from jax.sharding import PartitionSpec as P

RMIN = 2.0
BETA = 8.0
EMIN = 0.05
PENALTY = 4.0


def with_halo(array, sides, width):
    for axis, dim in sides:
        size, length = (lax.axis_size(axis), array.shape[dim])
        up = [(i, (i + 1) % size) for i in range(size - 1)]
        down = [(j, i) for i, j in up]
        last = lax.slice_in_dim(array, length - width, length, axis=dim)
        first = lax.slice_in_dim(array, 0, width, axis=dim)
        before = lax.ppermute(last, axis, up)
        after = lax.ppermute(first, axis, down)
        array = jnp.concatenate([before, array, after], axis=dim)
    return array


def conic(padded):
    rows_x, rows_y, rows_z = padded.shape
    total = jnp.zeros((rows_x - 2, rows_y - 2, rows_z - 2), padded.dtype)
    for step_x in range(3):
        for step_y in range(3):
            for step_z in range(3):
                spread = (
                    (step_x - 1) * (step_x - 1)
                    + (step_y - 1) * (step_y - 1)
                    + (step_z - 1) * (step_z - 1)
                )
                weight = RMIN - math.sqrt(spread)
                total = (
                    total
                    + weight
                    * padded[
                        step_x : step_x + rows_x - 2,
                        step_y : step_y + rows_y - 2,
                        step_z : step_z + rows_z - 2,
                    ]
                )
    return total


def project(filtered, eta):
    bottom = jnp.tanh(BETA * eta) + jnp.tanh(BETA * (1.0 - eta))
    inner = jnp.tanh(BETA * (filtered - eta))
    return ((jnp.tanh(BETA * eta) + inner) / bottom, BETA * (1.0 - inner * inner) / bottom)


def neighbours(field_x):
    centre = field_x[1:-1]
    padded = jnp.pad(centre, ((0, 0), (1, 1), (1, 1)))
    others = [
        field_x[2:],
        field_x[:-2],
        padded[:, 2:, 1:-1],
        padded[:, :-2, 1:-1],
        padded[:, 1:-1, 2:],
        padded[:, 1:-1, :-2],
    ]
    return (centre, others)


def conductance(stiff_x):
    centre, others = neighbours(stiff_x)
    return [0.5 * (centre + other) for other in others]


def operate(links, field_x):
    centre, others = neighbours(field_x)
    total = jnp.zeros_like(centre)
    for link, other in zip(links, others):
        total = total + link * (centre - other)
    return total


def energy(field_x):
    centre, others = neighbours(field_x)
    total = jnp.zeros_like(centre)
    for other in others:
        total = total + (centre - other) * (centre - other)
    return -0.5 * total


def inside(start, count, limit):
    places = start + jnp.arange(count, dtype=jnp.int32)
    return ((places >= 0) & (places < limit)).astype(jnp.float32)


def extend(field):
    return with_halo(field, (("space", 0),), 1)


def total_of(values):
    return lax.psum(jnp.sum(values), "space")


def local(design, solid_mask, void_mask, load_mask, support_mask, thresholds, group_weight):
    fixed = jnp.where(solid_mask == 1, 1.0, jnp.where(void_mask == 1, 0.0, design))
    depth, width, thick = design.shape
    spot = lax.axis_index("space")
    layer = lax.axis_index("proj")
    span_x = depth * lax.axis_size("space")
    span_z = thick * lax.axis_size("proj")
    inside_x = inside(spot * depth - 2, depth + 4, span_x)
    rimmed = with_halo(fixed, (("proj", 2), ("space", 0)), 2)
    padded = jnp.pad(rimmed, ((0, 0), (1, 1), (0, 0)))
    inside_y = jnp.pad(jnp.ones((width,), jnp.float32), 1)
    inside_z = inside(layer * thick - 2, thick + 4, span_z)
    indicator = inside_x[:, None, None] * inside_y[None, :, None] * inside_z[None, None, :]
    weight_sum = conic(indicator)[:, :, 1:-1]
    ratio = conic(padded)[:, :, 1:-1] / jnp.maximum(weight_sum, 1.0)
    filtered = lax.all_gather(ratio, "proj", axis=2, tiled=True)
    eta = thresholds[0].astype(jnp.float32) / 1000.0
    value, slope = project(filtered, eta)
    edge = inside(spot * depth - 1, depth + 2, span_x)[:, None, None]
    stiff = (EMIN + (1.0 - EMIN) * value * value * value) * edge
    links = conductance(stiff)
    load = load_mask.astype(jnp.float32)
    support = support_mask.astype(jnp.float32)
    diag = sum(links) + PENALTY * support
    resid = load
    precond = resid / diag
    rz_now = total_of(resid * precond)
    first = extend(precond)
    image = operate(links, first)
    step_one = rz_now / total_of(precond * image)
    solution = step_one * first
    resid = resid - step_one * image
    precond = resid / diag
    rz_next = total_of(resid * precond)
    second = extend(precond + rz_next / rz_now * first[1:-1])
    image = operate(links, second)
    step_two = rz_next / total_of(second[1:-1] * image)
    solution = solution + step_two * second
    core_value = value[1:-1]
    local_terms = (
        group_weight[0]
        * energy(solution)
        * (3.0 * (1.0 - EMIN))
        * core_value
        * core_value
        * slope[1:-1]
    )
    return lax.psum_scatter(local_terms, "proj", scatter_dimension=2, tiled=True)


def solution(mesh):
    placed = (
        P("space", None, "proj"),
        P("space", None, "proj"),
        P("space", None, "proj"),
        P("space", None, None),
        P("space", None, None),
        P("proj"),
        P("proj"),
    )
    return jax.shard_map(
        local, mesh=mesh, in_specs=placed, out_specs=P("space", None, "proj"), check_vma=False
    )
```

profile of v0, /device:TPU:1, one launch (start us, length us, event | category | flops | bytes accessed | tf_op | source)
XLA Modules:
  0.0 2143.0 jit_solution(9396928075356666915)
XLA Ops:
  6.5 0.9 select_select_fusion
  7.5 11.4 collective-permute-start
  19.0 1.3 collective-permute-start.1
  20.5 0.1 broadcast_multiply_fusion
  20.6 0.3 slice_multiply_fusion
  21.0 1.0 fusion.36
  22.7 6.1 collective-permute-done.1
  29.0 5.7 collective-permute-start.2
  34.7 1.9 collective-permute-start.3
  36.7 5.7 collective-permute-done.3
  42.4 0.2 maximum_maximum_fusion
  42.7 1.3 fusion.23
  44.0 0.5 fusion.120
  44.6 21.3 all_gather.3
  65.8 0.1 fusion.1
  66.0 0.9 copy-done
  67.0 0.2 convert_divide_fusion
  67.2 1.9 collective-permute-start.4
  69.2 3.6 collective-permute-start.5
  72.8 0.4 collective-permute-done.4
  73.2 1.3 collective-permute-done.5
  74.4 1.0 multiply_reduce_fusion.1
  75.4 665.6 %all-reduce.6 = (f32[]{:T(128)}, f32[]{:T(128)}) all-reduce(f32[]{:T(128)} %get-tuple-element.6, f32[]{:T(128)} %get-tuple-element.5), channel_id=1, replica_groups=mesh['proj'=3,'space'=256] {'space'}, use_global_device_ids=true, to_apply=%region_1.2 | all-reduce | flops 2 | bytes 16 | tf_op jit(solution)/shard_map/psum | solution.py:102
  742.3 0.7 multiply_reduce_fusion
  743.0 670.5 %psum.30 = f32[]{:T(128)} all-reduce(f32[]{:T(128)} %multiply_reduce_fusion), channel_id=1, replica_groups=mesh['proj'=3,'space'=256] {'space'}, use_global_device_ids=true, to_apply=%region_5.6 | all-reduce | flops 1 | bytes 8 | tf_op jit(solution)/shard_map/psum | solution.py:102
  1414.8 2.6 collective-permute-start.6
  1417.4 3.0 collective-permute-start.7
  1421.1 1.0 collective-permute-done.7
  1422.0 1.0 fusion.117
  1423.0 663.6 %psum.31 = f32[]{:T(128)} all-reduce(f32[]{:T(128)} %fusion.117), channel_id=1, replica_groups=mesh['proj'=3,'space'=256] {'space'}, use_global_device_ids=true, to_apply=%region_7.8 | all-reduce | flops 1 | bytes 8 | tf_op jit(solution)/shard_map/psum | solution.py:102
  2088.0 0.9 fusion.51
  2088.9 47.3 %reduce-scatter.2.cloned.1.call-done = f32[2,64,128]{2,1,0:T(8,128)} async-done(((f32[2,64,384]{2,1,0:T(8,128)}), f32[2,64,128]{2,1,0:T(8,128)}) %reduce-scatter.2.cloned.1.call-update) | async-done | bytes 65552 | tf_op jit(solution)/shard_map/reduce_scatter | solution.py:152
  (23 shorter events, 0.8 us)
Async XLA Ops:
  6.5 2129.7 %reduce-scatter.2.cloned.1.call-start = ((), (), s32[]{:S(2)}) async-start(), calls=%async_computation.1 | async-start | bytes 262144 | tf_op jit(solution)/shard_map/reduce_scatter | solution.py:152
  7.5 15.2 collective-permute-start
  19.0 9.9 collective-permute-start.1
  29.0 7.7 collective-permute-start.2
  34.7 7.7 collective-permute-start.3
  66.0 0.9 copy-start
  66.0 1.0 copy-start.1
  67.2 5.9 collective-permute-start.4
  69.2 5.3 collective-permute-start.5
  1414.8 6.2 collective-permute-start.6
  1417.4 4.6 collective-permute-start.7
Sparse Core Ops, SparseCore 0:
  2089.1 47.0 reduce-scatter.1
where the time goes:
time: 2140 us
  blocking collectives  2020 us (94%)
  waiting for transfers between devices  61.7 us (3%)
  starting transfers between devices  31.5 us (1%)
    psum x3, blocking collectives, total_of(): return lax.psum(jnp.sum(values), 'space')  2000 us
    reduce_scatter x1, waiting for transfers between devices, local(): lax.psum_scatter(local_terms, 'proj', scatter_dimension=2, tiled=True)  47.3 us
  transfers between devices with their start and end apart: 9, of which 6 were waited for; matrix products, arithmetic and copies ran while one was open for 0% of the time, Pallas kernels for 0%

commit v1 on v0

v1 whole, which is shorter than its diff:
```python
import math

import jax
import jax.numpy as jnp
from jax import lax
from jax.experimental import pallas as pl
from jax.experimental.pallas import tpu as pltpu
from jax.sharding import PartitionSpec as P

RMIN = 2.0
BETA = 8.0
EMIN = 0.05
PENALTY = 4.0
MESH = pl.DeviceIdType.MESH
F32 = jnp.float32

NPROJ, NSPACE = 3, 256
NYC, NXC, NZLO, NCORE = 8, 4, 4, 2
NZC = NPROJ * NZLO
DEPTH, WIDTH, THICK = 2, 64, 128
GX, GZ = NSPACE * DEPTH, NPROJ * THICK

LO, HI = 16, 16 + THICK
ROWS = HI + 16
EDGE = 2.0 - math.sqrt(2.0)
CORNER = 2.0 - math.sqrt(3.0)
OWN = [(LO + i, 32) for i in range(0, THICK, 32)]
ALL = [(LO - 8, 8)] + OWN + [(HI, 8)]


def kernel(
    design, solid, void, load_in, support_in, eta_in, weight_in, out,
    raw, masks, fb, ls, ring, lr, sr, inm, inv, tw, tanhs, hh, cond, zz, idg, ww, uu, kk, rowa, rowb, rowc, done,
    in_sem, send_f, recv_f, send_e, recv_e, send_m, recv_m, send_t, recv_t,
    send_a, recv_a, send_b, recv_b, send_c, recv_c,
):
    me = lax.axis_index("space")
    slab = lax.axis_index("proj")
    core = me % NCORE
    zlo = (me // NCORE) % NZLO
    xc = (me // (NCORE * NZLO)) % NXC
    line_a = xc * NCORE + core
    line_z = slab * NZLO + zlo

    def space_at(step):
        return (me + (NSPACE + step)) % NSPACE

    def slab_at(step):
        return (slab + (NPROJ + step)) % NPROJ

    def at_a(step):
        other = (line_a + step) % (NXC * NCORE)
        return (slab, me + ((other // NCORE - xc) * (NCORE * NZLO) + (other % NCORE - core)))

    def at_b(step):
        return (slab, (me + step * (NSPACE // NYC)) % NSPACE)

    def at_c(step):
        other = (line_z + step) % NZC
        return (other // NZLO, me + (other % NZLO - zlo) * NCORE)

    near = (1, -1, 2, -2)
    halo = [(slab, space_at(d)) for d in near]
    halo += [(slab_at(e), space_at(d)) for d in (0,) + near for e in (1, -1)]
    partners = halo + [at_a(d) for d in range(1, 8)] + [at_b(d) for d in range(1, 8)] + [at_c(d) for d in range(1, 12)]

    barrier = pltpu.get_barrier_semaphore()
    for place in partners:
        pl.semaphore_signal(barrier, inc=1, device_id=place, device_id_type=MESH)

    loads = []
    for i, source in enumerate((design, solid, void)):
        target = raw if i == 0 else masks.at[i - 1]
        loads.append(pltpu.make_async_copy(source, target, in_sem.at[i]))
    for i, source in enumerate((load_in, support_in)):
        for j, step in enumerate((-1, 0, 1)):
            lane = pl.multiple_of(slab_at(step) * THICK, THICK)
            loads.append(
                pltpu.make_async_copy(source.at[:, :, pl.ds(lane, THICK)], masks.at[2 + 3 * i + j], in_sem.at[3 + 3 * i + j])
            )
    for item in loads:
        item.start()

    lane = lax.broadcasted_iota(jnp.int32, (1, 128), 1)
    cell_y = lane % WIDTH
    upper = lane >= WIDTH
    has_up = cell_y < WIDTH - 1
    has_down = cell_y > 0

    def y_up(v):
        return jnp.where(has_up, pltpu.roll(v, 127, 1), 0.0)

    def y_down(v):
        return jnp.where(has_down, pltpu.roll(v, 1, 1), 0.0)

    def swap(v):
        return pltpu.roll(v, WIDTH, 1)

    count_y = has_up.astype(F32) + has_down.astype(F32)
    for k in range(5):
        layer = jnp.where(upper, 1 + k, -k) + me * DEPTH
        in_x = ((layer >= 0) & (layer < GX)).astype(F32)
        count_x = (layer > 0).astype(F32) + (layer < GX - 1).astype(F32)
        for r0, n in ALL:
            z = slab * THICK + (r0 - LO) + lax.broadcasted_iota(jnp.int32, (n, 128), 0)
            in_z = ((z >= 0) & (z < GZ)).astype(F32)
            inm[k, r0 : r0 + n, :] = in_z * in_x
            if k < 4:
                count_z = (z > 0).astype(F32) + (z < GZ - 1).astype(F32)
                pair = count_y * count_z
                total = 2.0 + count_x + count_y + count_z
                total = total + EDGE * (count_x * (count_y + count_z) + pair) + CORNER * (count_x * pair)
                inv[k, r0 : r0 + n, :] = BETA / total

    eta = eta_in[0].astype(F32) / 1000.0
    row = lax.broadcasted_iota(jnp.int32, (8, 128), 0)
    tw[slab] = jnp.where(row == 0, eta, weight_in[0])

    for item in loads[:3]:
        item.wait()
    fixed = jnp.where(masks[0] == 1, 1.0, jnp.where(masks[1] == 1, 0.0, raw[...]))
    fb[2, LO:HI, :] = fixed.reshape(128, 128).T
    for item in loads[3:]:
        item.wait()
    for i in range(2):
        for j in range(3):
            turned = masks[2 + 3 * i + j].reshape(128, 128).astype(F32).T
            if j == 0:
                ls[1, i, LO - 8 : LO, :] = turned[120:, :]
            elif j == 1:
                ls[1, i, LO:HI, :] = turned
            else:
                ls[1, i, HI : HI + 8, :] = turned[:8, :]

    pl.semaphore_wait(barrier, len(partners))

    def remote(source, target, ssem, rsem, place):
        return pltpu.make_async_remote_copy(
            src_ref=source, dst_ref=target, send_sem=ssem, recv_sem=rsem, device_id=place, device_id_type=MESH
        )

    main, rims, marks, small = [], [], [], []
    for i, d in enumerate(near):
        main.append(
            remote(fb.at[2, pl.ds(LO, THICK), :], fb.at[2 - d, pl.ds(LO, THICK), :], send_f.at[i], recv_f.at[i], (slab, space_at(d)))
        )
    for i, d in enumerate((0,) + near):
        for j, e in enumerate((1, -1)):
            src, dst = (HI - 8, LO - 8) if e == 1 else (LO, HI)
            rims.append(
                remote(
                    fb.at[2, pl.ds(src, 8), :], fb.at[2 - d, pl.ds(dst, 8), :],
                    send_e.at[2 * i + j], recv_e.at[2 * i + j], (slab_at(e), space_at(d)),
                )
            )
    for i, d in enumerate((1, -1)):
        marks.append(
            remote(
                ls.at[1, :, pl.ds(LO - 8, THICK + 16), :], ls.at[1 - d, :, pl.ds(LO - 8, THICK + 16), :],
                send_m.at[i], recv_m.at[i], (slab, space_at(d)),
            )
        )
    for i, e in enumerate((1, -1)):
        small.append(remote(tw.at[slab], tw.at[slab], send_t.at[i], recv_t.at[i], (slab_at(e), me)))
    copies = main[:2] + small + rims + main[2:] + marks
    for item in copies:
        item.start()
    for item in main + small + rims:
        item.wait_recv()

    for r0, n in ALL:
        rows = slice(r0, r0 + n)
        ring[0, rows, :] = fb[2, rows, :] * inm[0, rows, :]
        p1, m1, p2, m2 = fb[3, rows, :], fb[1, rows, :], fb[4, rows, :], fb[0, rows, :]
        ring[1, rows, :] = swap(jnp.where(upper, m1, p1)) * inm[1, rows, :]
        ring[2, rows, :] = jnp.where(upper, p1, m1) * inm[2, rows, :]
        ring[3, rows, :] = swap(jnp.where(upper, m2, p2)) * inm[3, rows, :]
        ring[4, rows, :] = jnp.where(upper, p2, m2) * inm[4, rows, :]

    etas, tops, scales, weights = [], [], [], []
    for g in range(NPROJ):
        e = tw[g, 0:1, :]
        t = jnp.tanh(BETA * e)
        bottom = t + jnp.tanh(BETA * (1.0 - e))
        etas.append(BETA * e)
        tops.append(t / bottom)
        scales.append(1.0 / bottom)
        weights.append(tw[g, 1:2, :] * (-0.5 * 3.0 * (1.0 - EMIN) * BETA) / bottom)

    for r0, n in ALL:
        rows = slice(r0, r0 + n)
        centre, side = [], []
        for k in range(5):
            v = ring[k, rows, :]
            zb = ring[k, r0 + 1 : r0 + n + 1, :] + ring[k, r0 - 1 : r0 + n - 1, :]
            yb = y_up(v) + y_down(v)
            cross = y_up(zb) + y_down(zb)
            faces = zb + yb
            if k < 4:
                centre.append(2.0 * v + faces + EDGE * cross)
            side.append(v + EDGE * faces + CORNER * cross)
        for k in range(4):
            inner = side[k - 1] if k else swap(side[0])
            f8 = (centre[k] + (inner + side[k + 1])) * inv[k, rows, :]
            mask = inm[k, rows, :]
            for g in range(NPROJ):
                t = jnp.tanh(f8 - etas[g])
                value = t * scales[g] + tops[g]
                square = value * value
                hh[g, k, rows, :] = ((0.5 * (1.0 - EMIN)) * (square * value) + 0.5 * EMIN) * mask
                if k == 0 and LO <= r0 < HI:
                    kk[g, r0 - LO : r0 - LO + n, :] = (weights[g] * square) * (1.0 - t * t)

    for item in marks:
        item.wait_recv()

    for r0, n in ALL:
        rows = slice(r0, r0 + n)
        for k in range(3):
            mask = inm[k, rows, :]
            both = []
            for i in range(2):
                if k == 0:
                    both.append(ls[1, i, rows, :])
                elif k == 1:
                    both.append(swap(jnp.where(upper, ls[0, i, rows, :], ls[2, i, rows, :])))
                else:
                    both.append(jnp.where(upper, ls[2, i, rows, :], ls[0, i, rows, :]))
            lr[k, rows, :] = both[0] * mask
            sr[k, rows, :] = PENALTY * jnp.maximum(both[1], 1.0 - mask)

    for g in range(NPROJ):
        for k in range(3):
            for r0, n in ALL:
                rows = slice(r0, r0 + n)
                h = hh[g, k, rows, :]
                inner = hh[g, k - 1, rows, :] if k else swap(h)
                links = [
                    h + inner,
                    h + hh[g, k + 1, rows, :],
                    h + y_up(h),
                    h + y_down(h),
                    h + hh[g, k, r0 + 1 : r0 + n + 1, :],
                    h + hh[g, k, r0 - 1 : r0 + n - 1, :],
                ]
                diag = sr[k, rows, :]
                for i, link in enumerate(links):
                    diag = diag + link
                    if k < 2:
                        cond[g, k, i, rows, :] = link
                inverse = inm[k, rows, :] / diag
                zz[g, k, rows, :] = lr[k, rows, :] * inverse
                if k < 2:
                    idg[g, k, rows, :] = inverse

    def others(field, g, k, r0, n, v):
        rows = slice(r0, r0 + n)
        return [
            field[g, k - 1, rows, :] if k else swap(v),
            field[g, k + 1, rows, :],
            y_up(v),
            y_down(v),
            field[g, k, r0 + 1 : r0 + n + 1, :],
            field[g, k, r0 - 1 : r0 + n - 1, :],
        ]

    def operate(field, g, k, r0, n):
        v = field[g, k, r0 : r0 + n, :]
        total = None
        for i, other in enumerate(others(field, g, k, r0, n, v)):
            term = cond[g, k, i, r0 : r0 + n, :] * (v - other)
            total = term if total is None else total + term
        return v, total

    def fold(v):
        return jnp.sum(v.reshape(v.shape[0] // 8, 8, 128), axis=0)

    sums = [[jnp.zeros((8, 128), F32) for _ in range(4)] for _ in range(NPROJ)]
    for g in range(NPROJ):
        for k in range(2):
            for r0, n in ALL:
                rows = slice(r0, r0 + n)
                v, image = operate(zz, g, k, r0, n)
                w = image * idg[g, k, rows, :]
                ww[g, k, rows, :] = w
                if k == 0 and LO <= r0 < HI:
                    sums[g][0] = sums[g][0] + fold(v * lr[0, rows, :])
                    sums[g][1] = sums[g][1] + fold(v * image)
                    sums[g][2] = sums[g][2] + fold(w * image)
        for r0, n in OWN:
            w, image = operate(ww, g, 0, r0, n)
            sums[g][3] = sums[g][3] + fold(w * image)

    parts = jnp.concatenate([jnp.sum(sums[g][i], axis=0, keepdims=True) for i in range(4) for g in range(NPROJ)] + [jnp.zeros((4, 128), F32)], axis=0)
    totals = jnp.sum(parts, axis=1, keepdims=True)
    which = lax.broadcasted_iota(jnp.int32, (16, 128), 0)
    place = (which // NPROJ) * 32 + which % NPROJ
    spot = lax.broadcasted_iota(jnp.int32, (16, 128), 1)
    line = jnp.sum(jnp.where((spot == place) & (which < 12), totals, 0.0), axis=0, keepdims=True)

    def share(value, rows_ref, ssem, rsem, target, size):
        rows_ref[0] = value
        items = [remote(rows_ref.at[0], rows_ref.at[d], ssem.at[d], rsem.at[d], target(d)) for d in range(1, size)]
        for item in items:
            item.start()
        for item in items:
            item.wait_recv()
        total = rows_ref[0]
        for d in range(1, size):
            total = total + rows_ref[d]
        return total, items

    line, items_a = share(line, rowa, send_a, recv_a, at_a, NXC * NCORE)
    line, items_b = share(line, rowb, send_b, recv_b, at_b, NYC)
    line, items_c = share(line, rowc, send_c, recv_c, at_c, NZC)

    rz0, pq1 = line, pltpu.roll(line, 96, 1)
    qdq, wsw = pltpu.roll(line, 64, 1), pltpu.roll(line, 32, 1)
    step_one = rz0 / pq1
    rz1 = rz0 - 2.0 * step_one * pq1 + step_one * step_one * qdq
    grow = 1.0 + rz1 / rz0
    pq2 = grow * grow * pq1 - 2.0 * grow * step_one * qdq + step_one * step_one * wsw
    step_two = rz1 / pq2
    along = step_one + step_two * grow
    across = -step_one * step_two

    for g in range(NPROJ):
        one = jnp.broadcast_to(along[:, g : g + 1], (1, 128))
        two = jnp.broadcast_to(across[:, g : g + 1], (1, 128))
        for k in range(2):
            for r0, n in ALL if k == 0 else OWN:
                rows = slice(r0, r0 + n)
                uu[g, k, rows, :] = one * zz[g, k, rows, :] + two * ww[g, k, rows, :]
    for r0, n in OWN:
        result = None
        for g in range(NPROJ):
            v = uu[g, 0, r0 : r0 + n, :]
            total = None
            for other in others(uu, g, 0, r0, n, v):
                gap = v - other
                total = gap * gap if total is None else total + gap * gap
            term = kk[g, r0 - LO : r0 - LO + n, :] * total
            result = term if result is None else result + term
        done[r0 - LO : r0 - LO + n, :] = result
    out[...] = done[...].T.reshape(DEPTH, WIDTH, THICK)

    for item in copies + items_a + items_b + items_c:
        item.wait_send()


def local(design, solid_mask, void_mask, load_mask, support_mask, thresholds, group_weight):
    dma = pltpu.SemaphoreType.DMA
    return pl.pallas_call(
        kernel,
        out_shape=jax.ShapeDtypeStruct((DEPTH, WIDTH, THICK), F32),
        in_specs=[pl.BlockSpec(memory_space=pl.ANY)] * 5 + [pl.BlockSpec(memory_space=pltpu.SMEM)] * 2,
        out_specs=pl.BlockSpec(memory_space=pltpu.VMEM),
        scratch_shapes=[
            pltpu.VMEM((DEPTH, WIDTH, THICK), F32),
            pltpu.VMEM((8, DEPTH, WIDTH, THICK), jnp.int32),
            pltpu.VMEM((5, ROWS, 128), F32),
            pltpu.VMEM((3, 2, ROWS, 128), F32),
            pltpu.VMEM((5, ROWS, 128), F32),
            pltpu.VMEM((3, ROWS, 128), F32),
            pltpu.VMEM((3, ROWS, 128), F32),
            pltpu.VMEM((5, ROWS, 128), F32),
            pltpu.VMEM((4, ROWS, 128), F32),
            pltpu.VMEM((NPROJ, 8, 128), F32),
            pltpu.VMEM((8, 128), F32),
            pltpu.VMEM((NPROJ, 4, ROWS, 128), F32),
            pltpu.VMEM((NPROJ, 2, 6, ROWS, 128), F32),
            pltpu.VMEM((NPROJ, 3, ROWS, 128), F32),
            pltpu.VMEM((NPROJ, 2, ROWS, 128), F32),
            pltpu.VMEM((NPROJ, 2, ROWS, 128), F32),
            pltpu.VMEM((NPROJ, 2, ROWS, 128), F32),
            pltpu.VMEM((NPROJ, THICK, 128), F32),
            pltpu.VMEM((8, 1, 128), F32),
            pltpu.VMEM((8, 1, 128), F32),
            pltpu.VMEM((12, 1, 128), F32),
            pltpu.VMEM((THICK, 128), F32),
            dma((9,)),
            dma((4,)), dma((4,)),
            dma((10,)), dma((10,)),
            dma((2,)), dma((2,)),
            dma((2,)), dma((2,)),
            dma((8,)), dma((8,)),
            dma((8,)), dma((8,)),
            dma((12,)), dma((12,)),
        ],
        compiler_params=pltpu.CompilerParams(collective_id=0, has_side_effects=True),
    )(design, solid_mask, void_mask, load_mask, support_mask, thresholds, group_weight)


def solution(mesh):
    placed = (
        P("space", None, "proj"),
        P("space", None, "proj"),
        P("space", None, "proj"),
        P("space", None, None),
        P("space", None, None),
        P("proj"),
        P("proj"),
    )
    return jax.shard_map(
        local, mesh=mesh, in_specs=placed, out_specs=P("space", None, "proj"), check_vma=False
    )
```

time: 2140 us -> 51.5 us (0.02)
  blocking collectives: 2020 us -> 0 us
  waiting for transfers between devices: 61.7 us -> 0 us
  Pallas kernels: 0 us -> 48.1 us
  starting transfers between devices: 31.5 us -> 0 us
    psum x3 -> x0, blocking collectives: 2000 us -> none  [total_of(): return lax.psum(jnp.sum(values), 'space')]
    pallas_call x0 -> x1, Pallas kernels: none -> 48.1 us  [local(): pl.pallas_call(kernel, out_shape=jax.ShapeDtypeStruct((DEPTH, WIDTH, THIC...]
    reduce_scatter x1 -> x0, waiting for transfers between devices: 47.3 us -> none  [local(): lax.psum_scatter(local_terms, 'proj', scatter_dimension=2, tiled=True)]
    ppermute x8 -> x0, starting transfers between devices: 31.5 us -> none  [the longest x4 23.8 us: with_halo(): before = lax.ppermute(last, axis, up)]
  transfers between devices with their start and end apart: 9 -> 0, of which waited for: 6 -> 0; matrix products, arithmetic and copies ran while one was open for 0% -> 0% of each run, Pallas kernels for 0% -> 0%
where the time goes in v1:
time: 51.5 us; the launch traced here: 50.9 us
  Pallas kernels  48.1 us (93%)
  local copies, waits for them, and re-layouts  1.47 us (3%)
  between operations  1.3 us (3%)
    pallas_call x1, Pallas kernels, local(): pl.pallas_call(kernel, out_shape=jax.ShapeDtypeStruct((DEPTH, WIDTH, THIC...  48.1 us
    unnamed x1, local copies, waits for them, and re-layouts  1.47 us

profile of v1, /device:TPU:1, one launch (start us, length us, event | category | flops | bytes accessed | tf_op | source)
XLA Modules:
  0.0 50.9 jit_solution(5591835282396974845)
XLA Ops:
  1.3 48.1 %shard_map.73 = f32[2,64,128]{2,1,0:T(8,128)} custom-call(f32[2,64,128]{2,1,0:T(8,128)} %design.1, s32[2,64,128]{2,1,0:T(8,128)} %solid.1, s32[2,64,128]{2,1,0:T(8,128)} %void.1, s32[2,64,384]{2,1,0:T(8,128)} %load_in.1, s32[2,64,384]{2,1,0:T(8,128)} %support_in.1, s32[1]{0:T(128)S(6)} %copy.9.eta_in, f32[1]{0:T(128)S(6)} %copy.10.weight_in), custom_call_target="tpu_custom_call" | custom-call | tf_op jit(solution)/shard_map/pallas_call | solution.py:353
  49.4 1.5 %copy.11 = f32[2,64,128]{2,1,0:T(8,128)} copy(f32[2,64,128]{2,1,0:T(8,128)} %shard_map.73) | data formatting | bytes 131072

commit v2 on v1

--- a/solution.py
+++ b/solution.py
@@ -30,43 +30,22 @@
 
 def kernel(
     design, solid, void, load_in, support_in, eta_in, weight_in, out,
-    raw, masks, fb, ls, ring, lr, sr, inm, inv, tw, tanhs, hh, cond, zz, idg, ww, uu, kk, rowa, rowb, rowc, done,
+    raw, masks, fb, lt, ls, ring, lr, sr, inm, inv, tw, hh, cond, zz, idg, ww, uu, kk, rowp, rowz, done,
     in_sem, send_f, recv_f, send_e, recv_e, send_m, recv_m, send_t, recv_t,
-    send_a, recv_a, send_b, recv_b, send_c, recv_c,
+    send_p, recv_p, send_z, recv_z,
 ):
     me = lax.axis_index("space")
     slab = lax.axis_index("proj")
-    core = me % NCORE
-    zlo = (me // NCORE) % NZLO
-    xc = (me // (NCORE * NZLO)) % NXC
-    line_a = xc * NCORE + core
+    core = me & 1
+    zlo = (me >> 1) & 3
     line_z = slab * NZLO + zlo
+    inward = 1 - 2 * core
+    slab_up = jnp.where(slab == NPROJ - 1, 0, slab + 1)
+    slab_down = jnp.where(slab == 0, NPROJ - 1, slab - 1)
+    slabs = {0: slab, 1: slab_up, -1: slab_down}
 
     def space_at(step):
-        return (me + (NSPACE + step)) % NSPACE
-
-    def slab_at(step):
-        return (slab + (NPROJ + step)) % NPROJ
-
-    def at_a(step):
-        other = (line_a + step) % (NXC * NCORE)
-        return (slab, me + ((other // NCORE - xc) * (NCORE * NZLO) + (other % NCORE - core)))
-
-    def at_b(step):
-        return (slab, (me + step * (NSPACE // NYC)) % NSPACE)
-
-    def at_c(step):
-        other = (line_z + step) % NZC
-        return (other // NZLO, me + (other % NZLO - zlo) * NCORE)
-
-    near = (1, -1, 2, -2)
-    halo = [(slab, space_at(d)) for d in near]
-    halo += [(slab_at(e), space_at(d)) for d in (0,) + near for e in (1, -1)]
-    partners = halo + [at_a(d) for d in range(1, 8)] + [at_b(d) for d in range(1, 8)] + [at_c(d) for d in range(1, 12)]
-
-    barrier = pltpu.get_barrier_semaphore()
-    for place in partners:
-        pl.semaphore_signal(barrier, inc=1, device_id=place, device_id_type=MESH)
+        return (me + step) & (NSPACE - 1)
 
     loads = []
     for i, source in enumerate((design, solid, void)):
@@ -74,11 +53,39 @@
         loads.append(pltpu.make_async_copy(source, target, in_sem.at[i]))
     for i, source in enumerate((load_in, support_in)):
         for j, step in enumerate((-1, 0, 1)):
-            lane = pl.multiple_of(slab_at(step) * THICK, THICK)
+            lane = pl.multiple_of(slabs[step] * THICK, THICK)
             loads.append(
                 pltpu.make_async_copy(source.at[:, :, pl.ds(lane, THICK)], masks.at[2 + 3 * i + j], in_sem.at[3 + 3 * i + j])
             )
-    for item in loads:
+    for item in loads[:3]:
+        item.start()
+
+    near = (1, -1, 2, -2)
+    halo = [(slabs[e], space_at(d)) for d in near[::-1] + (0,) for e in (1, -1)]
+    halo += [(slab, space_at(d)) for d in near]
+    rows_y = [(me + (dy << 5)) & 0xE0 for dy in range(NYC)]
+    rows_x = [(me + (dx << 3)) & 0x18 for dx in range(NXC)]
+    low = me & 0x07
+    plane = sorted(
+        ((dy, dx) for dy in range(NYC) for dx in range(NXC) if dy or dx),
+        key=lambda p: -(min(p[0], NYC - p[0]) + min(p[1], NXC - p[1])),
+    )
+    plane = [(slab, rows_y[dy] + rows_x[dx] + low) for dy, dx in plane]
+    stack = sorted(((dz, dc) for dz in range(NZC) for dc in range(NCORE) if dz or dc), key=lambda p: -min(p[0], NZC - p[0]))
+    base = me & 0xF8
+    cores = (core, 1 - core)
+    levels = []
+    for dz in range(NZC):
+        z = line_z + dz
+        z = jnp.where(z >= NZC, z - NZC, z)
+        levels.append((z >> 2, base + ((z & 3) << 1)))
+    stack = [(levels[dz][0], levels[dz][1] + cores[dc]) for dz, dc in stack]
+    partners = halo + plane + stack
+
+    barrier = pltpu.get_barrier_semaphore()
+    for place in partners:
+        pl.semaphore_signal(barrier, inc=1, device_id=place, device_id_type=MESH)
+    for item in loads[3:]:
         item.start()
 
     lane = lax.broadcasted_iota(jnp.int32, (1, 128), 1)
@@ -95,6 +102,72 @@
 
     def swap(v):
         return pltpu.roll(v, WIDTH, 1)
+
+    eta = eta_in[0].astype(F32) / 1000.0
+    row = lax.broadcasted_iota(jnp.int32, (8, 128), 0)
+    tw[slab] = jnp.where(row == 0, eta, weight_in[0])
+
+    for item in loads[:3]:
+        item.wait()
+    fixed = jnp.where(masks[0] == 1, 1.0, jnp.where(masks[1] == 1, 0.0, raw[...]))
+    fb[2, LO:HI, :] = fixed.reshape(128, 128).T
+
+    def remote(source, target, ssem, rsem, place):
+        return pltpu.make_async_remote_copy(
+            src_ref=source, dst_ref=target, send_sem=ssem, recv_sem=rsem, device_id=place, device_id_type=MESH
+        )
+
+    def main_copy(i, source, target, step):
+        return remote(
+            fb.at[source, pl.ds(LO, THICK), :], fb.at[target, pl.ds(LO, THICK), :],
+            send_f.at[i], recv_f.at[i], (slab, space_at(step)),
+        )
+
+    from_outer = main_copy(0, 2, 2 + inward, -inward)
+    from_far = main_copy(1, 2, 2 - 2 * inward, 2 * inward)
+    from_partner = main_copy(2, 2, 2 - inward, inward)
+    relay = main_copy(3, 2 - inward, 2 - 2 * inward, inward)
+    rims, marks, small = [], [], []
+    for i, d in enumerate(near[::-1] + (0,)):
+        for j, e in enumerate((1, -1)):
+            src, dst = (HI - 8, LO - 8) if e == 1 else (LO, HI)
+            rims.append(
+                remote(
+                    fb.at[2, pl.ds(src, 8), :], fb.at[2 - d, pl.ds(dst, 8), :],
+                    send_e.at[2 * i + j], recv_e.at[2 * i + j], (slabs[e], space_at(d)),
+                )
+            )
+    for i, e in enumerate((1, -1)):
+        small.append(remote(tw.at[slab], tw.at[slab], send_t.at[i], recv_t.at[i], (slabs[e], me)))
+
+    spill_up = ((me & 7) == 7).astype(jnp.int32)
+    spill_down = ((me & 7) == 0).astype(jnp.int32)
+    for i, (d, spill) in enumerate(((1, spill_up), (-1, -spill_down))):
+        start = pl.multiple_of(THICK + THICK * spill, 8)
+        place = jnp.where(spill == 0, slab, slabs[d])
+        marks.append(
+            remote(
+                lt.at[:, pl.ds(start, THICK + 16), :], ls.at[i, :, pl.ds(LO - 8, THICK + 16), :],
+                send_m.at[i], recv_m.at[i], (place, space_at(d)),
+            )
+        )
+
+    pl.semaphore_wait(barrier, len(partners))
+    for item in rims[:8] + [from_outer, from_far, from_partner] + rims[8:] + small:
+        item.start()
+
+    for item in loads[3:]:
+        item.wait()
+    for i in range(2):
+        for j in range(3):
+            turned = masks[2 + 3 * i + j].reshape(128, 128).astype(F32).T
+            lt[i, 8 + THICK * j : 8 + THICK * (j + 1), :] = turned
+            if j == 0:
+                lt[i, 8 + 3 * THICK :, :] = turned[:8, :]
+            if j == 2:
+                lt[i, 0:8, :] = turned[120:, :]
+    for item in marks:
+        item.start()
 
     count_y = has_up.astype(F32) + has_down.astype(F32)
     for k in range(5):
@@ -112,61 +185,11 @@
                 total = total + EDGE * (count_x * (count_y + count_z) + pair) + CORNER * (count_x * pair)
                 inv[k, r0 : r0 + n, :] = BETA / total
 
-    eta = eta_in[0].astype(F32) / 1000.0
-    row = lax.broadcasted_iota(jnp.int32, (8, 128), 0)
-    tw[slab] = jnp.where(row == 0, eta, weight_in[0])
-
-    for item in loads[:3]:
-        item.wait()
-    fixed = jnp.where(masks[0] == 1, 1.0, jnp.where(masks[1] == 1, 0.0, raw[...]))
-    fb[2, LO:HI, :] = fixed.reshape(128, 128).T
-    for item in loads[3:]:
-        item.wait()
-    for i in range(2):
-        for j in range(3):
-            turned = masks[2 + 3 * i + j].reshape(128, 128).astype(F32).T
-            if j == 0:
-                ls[1, i, LO - 8 : LO, :] = turned[120:, :]
-            elif j == 1:
-                ls[1, i, LO:HI, :] = turned
-            else:
-                ls[1, i, HI : HI + 8, :] = turned[:8, :]
-
-    pl.semaphore_wait(barrier, len(partners))
-
-    def remote(source, target, ssem, rsem, place):
-        return pltpu.make_async_remote_copy(
-            src_ref=source, dst_ref=target, send_sem=ssem, recv_sem=rsem, device_id=place, device_id_type=MESH
-        )
-
-    main, rims, marks, small = [], [], [], []
-    for i, d in enumerate(near):
-        main.append(
-            remote(fb.at[2, pl.ds(LO, THICK), :], fb.at[2 - d, pl.ds(LO, THICK), :], send_f.at[i], recv_f.at[i], (slab, space_at(d)))
-        )
-    for i, d in enumerate((0,) + near):
-        for j, e in enumerate((1, -1)):
-            src, dst = (HI - 8, LO - 8) if e == 1 else (LO, HI)
-            rims.append(
-                remote(
-                    fb.at[2, pl.ds(src, 8), :], fb.at[2 - d, pl.ds(dst, 8), :],
-                    send_e.at[2 * i + j], recv_e.at[2 * i + j], (slab_at(e), space_at(d)),
-                )
-            )
-    for i, d in enumerate((1, -1)):
-        marks.append(
-            remote(
-                ls.at[1, :, pl.ds(LO - 8, THICK + 16), :], ls.at[1 - d, :, pl.ds(LO - 8, THICK + 16), :],
-                send_m.at[i], recv_m.at[i], (slab, space_at(d)),
-            )
-        )
-    for i, e in enumerate((1, -1)):
-        small.append(remote(tw.at[slab], tw.at[slab], send_t.at[i], recv_t.at[i], (slab_at(e), me)))
-    copies = main[:2] + small + rims + main[2:] + marks
-    for item in copies:
-        item.start()
-    for item in main + small + rims:
+    from_outer.wait_recv()
+    relay.start()
+    for item in [from_far, from_partner] + small + rims:
         item.wait_recv()
+    relay.wait_recv()
 
     for r0, n in ALL:
         rows = slice(r0, r0 + n)
@@ -221,11 +244,11 @@
             both = []
             for i in range(2):
                 if k == 0:
-                    both.append(ls[1, i, rows, :])
+                    both.append(lt[i, r0 + 8 + THICK - LO : r0 + n + 8 + THICK - LO, :])
                 elif k == 1:
-                    both.append(swap(jnp.where(upper, ls[0, i, rows, :], ls[2, i, rows, :])))
+                    both.append(swap(jnp.where(upper, ls[0, i, rows, :], ls[1, i, rows, :])))
                 else:
-                    both.append(jnp.where(upper, ls[2, i, rows, :], ls[0, i, rows, :]))
+                    both.append(jnp.where(upper, ls[1, i, rows, :], ls[0, i, rows, :]))
             lr[k, rows, :] = both[0] * mask
             sr[k, rows, :] = PENALTY * jnp.maximum(both[1], 1.0 - mask)
 
@@ -298,21 +321,27 @@
     spot = lax.broadcasted_iota(jnp.int32, (16, 128), 1)
     line = jnp.sum(jnp.where((spot == place) & (which < 12), totals, 0.0), axis=0, keepdims=True)
 
-    def share(value, rows_ref, ssem, rsem, target, size):
+    def share(value, rows_ref, ssem, rsem, places):
         rows_ref[0] = value
-        items = [remote(rows_ref.at[0], rows_ref.at[d], ssem.at[d], rsem.at[d], target(d)) for d in range(1, size)]
-        for item in items:
-            item.start()
-        for item in items:
-            item.wait_recv()
-        total = rows_ref[0]
-        for d in range(1, size):
-            total = total + rows_ref[d]
-        return total, items
-
-    line, items_a = share(line, rowa, send_a, recv_a, at_a, NXC * NCORE)
-    line, items_b = share(line, rowb, send_b, recv_b, at_b, NYC)
-    line, items_c = share(line, rowc, send_c, recv_c, at_c, NZC)
+        for d, place in enumerate(places):
+            remote(rows_ref.at[0], rows_ref.at[d + 1], ssem.at[0], rsem.at[0], place).start()
+        every = rows_ref.at[pl.ds(1, len(places))]
+        return remote(every, every, ssem.at[0], rsem.at[0], places[0])
+
+    def gathered(rows_ref, size):
+        terms = [rows_ref[d] for d in range(size)]
+        while len(terms) > 1:
+            terms = [a + b for a, b in zip(terms[::2], terms[1::2])] + terms[len(terms) // 2 * 2 :]
+        return terms[0]
+
+    in_plane = share(line, rowp, send_p, recv_p, plane)
+    for item in [from_outer, from_far, from_partner, relay] + rims + small + marks:
+        item.wait_send()
+    in_plane.wait_recv()
+    in_stack = share(gathered(rowp, NXC * NYC), rowz, send_z, recv_z, stack)
+    in_plane.wait_send()
+    in_stack.wait_recv()
+    line = gathered(rowz, NZC * NCORE)
 
     rz0, pq1 = line, pltpu.roll(line, 96, 1)
     qdq, wsw = pltpu.roll(line, 64, 1), pltpu.roll(line, 32, 1)
@@ -344,8 +373,7 @@
         done[r0 - LO : r0 - LO + n, :] = result
     out[...] = done[...].T.reshape(DEPTH, WIDTH, THICK)
 
-    for item in copies + items_a + items_b + items_c:
-        item.wait_send()
+    in_stack.wait_send()
 
 
 def local(design, solid_mask, void_mask, load_mask, support_mask, thresholds, group_weight):
@@ -359,14 +387,14 @@
             pltpu.VMEM((DEPTH, WIDTH, THICK), F32),
             pltpu.VMEM((8, DEPTH, WIDTH, THICK), jnp.int32),
             pltpu.VMEM((5, ROWS, 128), F32),
-            pltpu.VMEM((3, 2, ROWS, 128), F32),
+            pltpu.VMEM((2, 3 * THICK + 16, 128), F32),
+            pltpu.VMEM((2, 2, ROWS, 128), F32),
             pltpu.VMEM((5, ROWS, 128), F32),
             pltpu.VMEM((3, ROWS, 128), F32),
             pltpu.VMEM((3, ROWS, 128), F32),
             pltpu.VMEM((5, ROWS, 128), F32),
             pltpu.VMEM((4, ROWS, 128), F32),
             pltpu.VMEM((NPROJ, 8, 128), F32),
-            pltpu.VMEM((8, 128), F32),
             pltpu.VMEM((NPROJ, 4, ROWS, 128), F32),
             pltpu.VMEM((NPROJ, 2, 6, ROWS, 128), F32),
             pltpu.VMEM((NPROJ, 3, ROWS, 128), F32),
@@ -374,18 +402,16 @@
             pltpu.VMEM((NPROJ, 2, ROWS, 128), F32),
             pltpu.VMEM((NPROJ, 2, ROWS, 128), F32),
             pltpu.VMEM((NPROJ, THICK, 128), F32),
-            pltpu.VMEM((8, 1, 128), F32),
-            pltpu.VMEM((8, 1, 128), F32),
-            pltpu.VMEM((12, 1, 128), F32),
+            pltpu.VMEM((NXC * NYC, 1, 128), F32),
+            pltpu.VMEM((NZC * NCORE, 1, 128), F32),
             pltpu.VMEM((THICK, 128), F32),
             dma((9,)),
             dma((4,)), dma((4,)),
             dma((10,)), dma((10,)),
             dma((2,)), dma((2,)),
             dma((2,)), dma((2,)),
-            dma((8,)), dma((8,)),
-            dma((8,)), dma((8,)),
-            dma((12,)), dma((12,)),
+            dma((1,)), dma((1,)),
+            dma((1,)), dma((1,)),
         ],
         compiler_params=pltpu.CompilerParams(collective_id=0, has_side_effects=True),
     )(design, solid_mask, void_mask, load_mask, support_mask, thresholds, group_weight)

time: 51.5 us -> 47.2 us (0.917)
  Pallas kernels: 48.1 us -> 44.2 us
    pallas_call x1, Pallas kernels: 48.1 us -> 44.2 us  [local(): pl.pallas_call(kernel, out_shape=jax.ShapeDtypeStruct((DEPTH, WIDTH, THIC...]
where the time goes in v2:
time: 47.2 us; the launch traced here: 47 us
  Pallas kernels  44.2 us (94%)
  local copies, waits for them, and re-layouts  1.47 us (3%)
  between operations  1.3 us (3%)
    pallas_call x1, Pallas kernels, local(): pl.pallas_call(kernel, out_shape=jax.ShapeDtypeStruct((DEPTH, WIDTH, THIC...  44.2 us
    unnamed x1, local copies, waits for them, and re-layouts  1.47 us

profile of v2, /device:TPU:1, one launch (start us, length us, event | category | flops | bytes accessed | tf_op | source)
XLA Modules:
  0.0 47.0 jit_solution(5617952702913863741)
XLA Ops:
  1.3 44.2 %shard_map.73 = f32[2,64,128]{2,1,0:T(8,128)} custom-call(f32[2,64,128]{2,1,0:T(8,128)} %design.1, s32[2,64,128]{2,1,0:T(8,128)} %solid.1, s32[2,64,128]{2,1,0:T(8,128)} %void.1, s32[2,64,384]{2,1,0:T(8,128)} %load_in.1, s32[2,64,384]{2,1,0:T(8,128)} %support_in.1, s32[1]{0:T(128)S(6)} %copy.9.eta_in, f32[1]{0:T(128)S(6)} %copy.10.weight_in), custom_call_target="tpu_custom_call" | custom-call | tf_op jit(solution)/shard_map/pallas_call | solution.py:381
  45.5 1.5 %copy.11 = f32[2,64,128]{2,1,0:T(8,128)} copy(f32[2,64,128]{2,1,0:T(8,128)} %shard_map.73) | data formatting | bytes 131072

commit v3 on v2

--- a/solution.py
+++ b/solution.py
@@ -25,12 +25,17 @@
 EDGE = 2.0 - math.sqrt(2.0)
 CORNER = 2.0 - math.sqrt(3.0)
 OWN = [(LO + i, 32) for i in range(0, THICK, 32)]
-ALL = [(LO - 8, 8)] + OWN + [(HI, 8)]
+RIM = [(LO - 8, 8), (HI, 8)]
+ALL = RIM[:1] + OWN + RIM[1:]
+FILTER = [(24, 40), (64, 40), (104, 32)], [(8, 16), (136, 16)]
+DIAGONAL = [(32, 32), (64, 32), (96, 32)], [(8, 24), (128, 24)]
+FIRST = [(40, 40), (80, 40)], [(8, 32), (120, 32)]
+SECOND = [(48, 32), (80, 32)], [(16, 32), (112, 32)]
 
 
 def kernel(
     design, solid, void, load_in, support_in, eta_in, weight_in, out,
-    raw, masks, fb, lt, ls, ring, lr, sr, inm, inv, tw, hh, cond, zz, idg, ww, uu, kk, rowp, rowz, done,
+    raw, masks, fb, lt, ls, ring, lr, sr, inm, inv, tw, hh, cond, zz, idg, ww, kk, rowp, rowz, ee, turned_e,
     in_sem, send_f, recv_f, send_e, recv_e, send_m, recv_m, send_t, recv_t,
     send_p, recv_p, send_z, recv_z,
 ):
@@ -187,18 +192,21 @@
 
     from_outer.wait_recv()
     relay.start()
-    for item in [from_far, from_partner] + small + rims:
+    for item in [from_partner, from_far] + small:
         item.wait_recv()
     relay.wait_recv()
 
-    for r0, n in ALL:
-        rows = slice(r0, r0 + n)
-        ring[0, rows, :] = fb[2, rows, :] * inm[0, rows, :]
-        p1, m1, p2, m2 = fb[3, rows, :], fb[1, rows, :], fb[4, rows, :], fb[0, rows, :]
-        ring[1, rows, :] = swap(jnp.where(upper, m1, p1)) * inm[1, rows, :]
-        ring[2, rows, :] = jnp.where(upper, p1, m1) * inm[2, rows, :]
-        ring[3, rows, :] = swap(jnp.where(upper, m2, p2)) * inm[3, rows, :]
-        ring[4, rows, :] = jnp.where(upper, p2, m2) * inm[4, rows, :]
+    def form_rings(chunks):
+        for r0, n in chunks:
+            rows = slice(r0, r0 + n)
+            ring[0, rows, :] = fb[2, rows, :] * inm[0, rows, :]
+            p1, m1, p2, m2 = fb[3, rows, :], fb[1, rows, :], fb[4, rows, :], fb[0, rows, :]
+            ring[1, rows, :] = swap(jnp.where(upper, m1, p1)) * inm[1, rows, :]
+            ring[2, rows, :] = jnp.where(upper, p1, m1) * inm[2, rows, :]
+            ring[3, rows, :] = swap(jnp.where(upper, m2, p2)) * inm[3, rows, :]
+            ring[4, rows, :] = jnp.where(upper, p2, m2) * inm[4, rows, :]
+
+    form_rings(OWN)
 
     etas, tops, scales, weights = [], [], [], []
     for g in range(NPROJ):
@@ -210,29 +218,102 @@
         scales.append(1.0 / bottom)
         weights.append(tw[g, 1:2, :] * (-0.5 * 3.0 * (1.0 - EMIN) * BETA) / bottom)
 
-    for r0, n in ALL:
+    def project(chunks):
+        for r0, n in chunks:
+            rows = slice(r0, r0 + n)
+            centre, side = [], []
+            for k in range(5):
+                v = ring[k, rows, :]
+                zb = ring[k, r0 + 1 : r0 + n + 1, :] + ring[k, r0 - 1 : r0 + n - 1, :]
+                yb = y_up(v) + y_down(v)
+                cross = y_up(zb) + y_down(zb)
+                faces = zb + yb
+                if k < 4:
+                    centre.append(2.0 * v + faces + EDGE * cross)
+                side.append(v + EDGE * faces + CORNER * cross)
+            for k in range(4):
+                inner = side[k - 1] if k else swap(side[0])
+                f8 = (centre[k] + (inner + side[k + 1])) * inv[k, rows, :]
+                mask = inm[k, rows, :]
+                for g in range(NPROJ):
+                    t = jnp.tanh(f8 - etas[g])
+                    value = t * scales[g] + tops[g]
+                    square = value * value
+                    hh[g, k, rows, :] = ((0.5 * (1.0 - EMIN)) * (square * value) + 0.5 * EMIN) * mask
+                    if k == 0:
+                        kk[g, rows, :] = (weights[g] * square) * (1.0 - t * t)
+
+    def precondition(chunks):
+        for g in range(NPROJ):
+            for k in range(3):
+                for r0, n in chunks:
+                    rows = slice(r0, r0 + n)
+                    h = hh[g, k, rows, :]
+                    inner = hh[g, k - 1, rows, :] if k else swap(h)
+                    links = [
+                        h + inner,
+                        h + hh[g, k + 1, rows, :],
+                        h + y_up(h),
+                        h + y_down(h),
+                        h + hh[g, k, r0 + 1 : r0 + n + 1, :],
+                        h + hh[g, k, r0 - 1 : r0 + n - 1, :],
+                    ]
+                    diag = sr[k, rows, :]
+                    for i, link in enumerate(links):
+                        diag = diag + link
+                        if k < 2:
+                            cond[g, k, i, rows, :] = link
+                    inverse = inm[k, rows, :] / diag
+                    zz[g, k, rows, :] = lr[k, rows, :] * inverse
+                    if k < 2:
+                        idg[g, k, rows, :] = inverse
+
+    def others(field, g, k, r0, n, v):
         rows = slice(r0, r0 + n)
-        centre, side = [], []
-        for k in range(5):
-            v = ring[k, rows, :]
-            zb = ring[k, r0 + 1 : r0 + n + 1, :] + ring[k, r0 - 1 : r0 + n - 1, :]
-            yb = y_up(v) + y_down(v)
-            cross = y_up(zb) + y_down(zb)
-            faces = zb + yb
-            if k < 4:
-                centre.append(2.0 * v + faces + EDGE * cross)
-            side.append(v + EDGE * faces + CORNER * cross)
-        for k in range(4):
-            inner = side[k - 1] if k else swap(side[0])
-            f8 = (centre[k] + (inner + side[k + 1])) * inv[k, rows, :]
-            mask = inm[k, rows, :]
-            for g in range(NPROJ):
-                t = jnp.tanh(f8 - etas[g])
-                value = t * scales[g] + tops[g]
-                square = value * value
-                hh[g, k, rows, :] = ((0.5 * (1.0 - EMIN)) * (square * value) + 0.5 * EMIN) * mask
-                if k == 0 and LO <= r0 < HI:
-                    kk[g, r0 - LO : r0 - LO + n, :] = (weights[g] * square) * (1.0 - t * t)
+        return [
+            field[g, k - 1, rows, :] if k else swap(v),
+            field[g, k + 1, rows, :],
+            y_up(v),
+            y_down(v),
+            field[g, k, r0 + 1 : r0 + n + 1, :],
+            field[g, k, r0 - 1 : r0 + n - 1, :],
+        ]
+
+    def operate(field, g, k, r0, n):
+        v = field[g, k, r0 : r0 + n, :]
+        total = None
+        for i, other in enumerate(others(field, g, k, r0, n, v)):
+            term = cond[g, k, i, r0 : r0 + n, :] * (v - other)
+            total = term if total is None else total + term
+        return v, total
+
+    sums = [[None] * 4 for _ in range(NPROJ)]
+
+    def add(g, i, r0, n, v):
+        v = v[max(LO - r0, 0) : n - max(r0 + n - HI, 0)]
+        v = jnp.sum(v.reshape(v.shape[0] // 8, 8, 128), axis=0)
+        sums[g][i] = v if sums[g][i] is None else sums[g][i] + v
+
+    def first_step(chunks):
+        for g in range(NPROJ):
+            for k in range(2):
+                for r0, n in chunks:
+                    rows = slice(r0, r0 + n)
+                    v, image = operate(zz, g, k, r0, n)
+                    w = image * idg[g, k, rows, :]
+                    ww[g, k, rows, :] = w
+                    if k == 0:
+                        add(g, 0, r0, n, v * lr[0, rows, :])
+                        add(g, 1, r0, n, v * image)
+                        add(g, 2, r0, n, w * image)
+
+    def second_step(chunks):
+        for g in range(NPROJ):
+            for r0, n in chunks:
+                w, image = operate(ww, g, 0, r0, n)
+                add(g, 3, r0, n, w * image)
+
+    project(FILTER[0])
 
     for item in marks:
         item.wait_recv()
@@ -252,67 +333,17 @@
             lr[k, rows, :] = both[0] * mask
             sr[k, rows, :] = PENALTY * jnp.maximum(both[1], 1.0 - mask)
 
-    for g in range(NPROJ):
-        for k in range(3):
-            for r0, n in ALL:
-                rows = slice(r0, r0 + n)
-                h = hh[g, k, rows, :]
-                inner = hh[g, k - 1, rows, :] if k else swap(h)
-                links = [
-                    h + inner,
-                    h + hh[g, k + 1, rows, :],
-                    h + y_up(h),
-                    h + y_down(h),
-                    h + hh[g, k, r0 + 1 : r0 + n + 1, :],
-                    h + hh[g, k, r0 - 1 : r0 + n - 1, :],
-                ]
-                diag = sr[k, rows, :]
-                for i, link in enumerate(links):
-                    diag = diag + link
-                    if k < 2:
-                        cond[g, k, i, rows, :] = link
-                inverse = inm[k, rows, :] / diag
-                zz[g, k, rows, :] = lr[k, rows, :] * inverse
-                if k < 2:
-                    idg[g, k, rows, :] = inverse
-
-    def others(field, g, k, r0, n, v):
-        rows = slice(r0, r0 + n)
-        return [
-            field[g, k - 1, rows, :] if k else swap(v),
-            field[g, k + 1, rows, :],
-            y_up(v),
-            y_down(v),
-            field[g, k, r0 + 1 : r0 + n + 1, :],
-            field[g, k, r0 - 1 : r0 + n - 1, :],
-        ]
-
-    def operate(field, g, k, r0, n):
-        v = field[g, k, r0 : r0 + n, :]
-        total = None
-        for i, other in enumerate(others(field, g, k, r0, n, v)):
-            term = cond[g, k, i, r0 : r0 + n, :] * (v - other)
-            total = term if total is None else total + term
-        return v, total
-
-    def fold(v):
-        return jnp.sum(v.reshape(v.shape[0] // 8, 8, 128), axis=0)
-
-    sums = [[jnp.zeros((8, 128), F32) for _ in range(4)] for _ in range(NPROJ)]
-    for g in range(NPROJ):
-        for k in range(2):
-            for r0, n in ALL:
-                rows = slice(r0, r0 + n)
-                v, image = operate(zz, g, k, r0, n)
-                w = image * idg[g, k, rows, :]
-                ww[g, k, rows, :] = w
-                if k == 0 and LO <= r0 < HI:
-                    sums[g][0] = sums[g][0] + fold(v * lr[0, rows, :])
-                    sums[g][1] = sums[g][1] + fold(v * image)
-                    sums[g][2] = sums[g][2] + fold(w * image)
-        for r0, n in OWN:
-            w, image = operate(ww, g, 0, r0, n)
-            sums[g][3] = sums[g][3] + fold(w * image)
+    precondition(DIAGONAL[0])
+    first_step(FIRST[0])
+    second_step(SECOND[0])
+
+    for item in rims:
+        item.wait_recv()
+    form_rings(RIM)
+    project(FILTER[1])
+    precondition(DIAGONAL[1])
+    first_step(FIRST[1])
+    second_step(SECOND[1])
 
     parts = jnp.concatenate([jnp.sum(sums[g][i], axis=0, keepdims=True) for i in range(4) for g in range(NPROJ)] + [jnp.zeros((4, 128), F32)], axis=0)
     totals = jnp.sum(parts, axis=1, keepdims=True)
@@ -337,6 +368,21 @@
     in_plane = share(line, rowp, send_p, recv_p, plane)
     for item in [from_outer, from_far, from_partner, relay] + rims + small + marks:
         item.wait_send()
+
+    for g in range(NPROJ):
+        for r0, n in OWN:
+            rows = slice(r0, r0 + n)
+            v, w = zz[g, 0, rows, :], ww[g, 0, rows, :]
+            forms = [None] * 3
+            for a, b in zip(others(zz, g, 0, r0, n, v), others(ww, g, 0, r0, n, w)):
+                gap_v, gap_w = v - a, w - b
+                for i, term in enumerate((gap_v * gap_v, gap_v * gap_w, gap_w * gap_w)):
+                    forms[i] = term if forms[i] is None else forms[i] + term
+            for i in range(3):
+                ee[g, i, r0 - LO : r0 - LO + n, :] = forms[i] * kk[g, rows, :]
+        for i in range(3):
+            turned_e[g, i] = ee[g, i].T
+
     in_plane.wait_recv()
     in_stack = share(gathered(rowp, NXC * NYC), rowz, send_z, recv_z, stack)
     in_plane.wait_send()
@@ -353,25 +399,17 @@
     along = step_one + step_two * grow
     across = -step_one * step_two
 
-    for g in range(NPROJ):
-        one = jnp.broadcast_to(along[:, g : g + 1], (1, 128))
-        two = jnp.broadcast_to(across[:, g : g + 1], (1, 128))
-        for k in range(2):
-            for r0, n in ALL if k == 0 else OWN:
-                rows = slice(r0, r0 + n)
-                uu[g, k, rows, :] = one * zz[g, k, rows, :] + two * ww[g, k, rows, :]
-    for r0, n in OWN:
-        result = None
-        for g in range(NPROJ):
-            v = uu[g, 0, r0 : r0 + n, :]
-            total = None
-            for other in others(uu, g, 0, r0, n, v):
-                gap = v - other
-                total = gap * gap if total is None else total + gap * gap
-            term = kk[g, r0 - LO : r0 - LO + n, :] * total
-            result = term if result is None else result + term
-        done[r0 - LO : r0 - LO + n, :] = result
-    out[...] = done[...].T.reshape(DEPTH, WIDTH, THICK)
+    scale = (along * along, 2.0 * along * across, across * across)
+    factors = [[jnp.broadcast_to(part[:, g : g + 1], (1, 128)) for part in scale] for g in range(NPROJ)]
+    for layer in range(DEPTH):
+        for y in range(0, WIDTH, 32):
+            rows = slice(layer * WIDTH + y, layer * WIDTH + y + 32)
+            result = None
+            for g in range(NPROJ):
+                for i in range(3):
+                    term = factors[g][i] * turned_e[g, i, rows, :]
+                    result = term if result is None else result + term
+            out[layer, y : y + 32, :] = result
 
     in_stack.wait_send()
 
@@ -380,7 +418,7 @@
     dma = pltpu.SemaphoreType.DMA
     return pl.pallas_call(
         kernel,
-        out_shape=jax.ShapeDtypeStruct((DEPTH, WIDTH, THICK), F32),
+        out_shape=pltpu.VMEM((DEPTH, WIDTH, THICK), F32),
         in_specs=[pl.BlockSpec(memory_space=pl.ANY)] * 5 + [pl.BlockSpec(memory_space=pltpu.SMEM)] * 2,
         out_specs=pl.BlockSpec(memory_space=pltpu.VMEM),
         scratch_shapes=[
@@ -400,11 +438,11 @@
             pltpu.VMEM((NPROJ, 3, ROWS, 128), F32),
             pltpu.VMEM((NPROJ, 2, ROWS, 128), F32),
             pltpu.VMEM((NPROJ, 2, ROWS, 128), F32),
-            pltpu.VMEM((NPROJ, 2, ROWS, 128), F32),
-            pltpu.VMEM((NPROJ, THICK, 128), F32),
+            pltpu.VMEM((NPROJ, ROWS, 128), F32),
             pltpu.VMEM((NXC * NYC, 1, 128), F32),
             pltpu.VMEM((NZC * NCORE, 1, 128), F32),
-            pltpu.VMEM((THICK, 128), F32),
+            pltpu.VMEM((NPROJ, 3, THICK, 128), F32),
+            pltpu.VMEM((NPROJ, 3, THICK, 128), F32),
             dma((9,)),
             dma((4,)), dma((4,)),
             dma((10,)), dma((10,)),

time: 47.2 us -> 45.6 us (0.966)
  local copies, waits for them, and re-layouts: 1.47 us -> 0.63 us
  Pallas kernels: 44.2 us -> 43.4 us
    unnamed x1, local copies, waits for them, and re-layouts: 1.47 us -> 0.63 us
    pallas_call x1, Pallas kernels: 44.2 us -> 43.4 us  [local(): pl.pallas_call(kernel, out_shape=pltpu.VMEM((DEPTH, WIDTH, THICK), F32),...]
where the time goes in v3:
time: 45.6 us; the launch traced here: 45.4 us
  Pallas kernels  43.4 us (95%)
  between operations  1.3 us (3%)
  local copies, waits for them, and re-layouts  0.63 us (1%)
    pallas_call x1, Pallas kernels, local(): pl.pallas_call(kernel, out_shape=pltpu.VMEM((DEPTH, WIDTH, THICK), F32),...  43.4 us

profile of v3, /device:TPU:1, one launch (start us, length us, event | category | flops | bytes accessed | tf_op | source)
XLA Modules:
  0.0 45.4 jit_solution(15519709670041998294)
XLA Ops:
  1.3 43.4 %shard_map.73 = f32[2,64,128]{2,1,0:T(8,128)S(1)} custom-call(f32[2,64,128]{2,1,0:T(8,128)} %design.1, s32[2,64,128]{2,1,0:T(8,128)} %solid.1, s32[2,64,128]{2,1,0:T(8,128)} %void.1, s32[2,64,384]{2,1,0:T(8,128)} %load_in.1, s32[2,64,384]{2,1,0:T(8,128)} %support_in.1, s32[1]{0:T(128)S(6)} %copy.10.eta_in, f32[1]{0:T(128)S(6)} %copy.11.weight_in), custom_call_target="tpu_custom_call" | custom-call | tf_op jit(solution)/shard_map/pallas_call | solution.py:419
  44.7 0.6 %copy.9 = f32[2,64,128]{2,1,0:T(8,128)} copy(f32[2,64,128]{2,1,0:T(8,128)S(1)} %shard_map.73) | data formatting | bytes 131072

commit v4 on v3

--- a/solution.py
+++ b/solution.py
@@ -25,8 +25,8 @@
 EDGE = 2.0 - math.sqrt(2.0)
 CORNER = 2.0 - math.sqrt(3.0)
 OWN = [(LO + i, 32) for i in range(0, THICK, 32)]
-RIM = [(LO - 8, 8), (HI, 8)]
-ALL = RIM[:1] + OWN + RIM[1:]
+ALL = [(LO - 8, 8)] + OWN + [(HI, 8)]
+REACH = 4
 FILTER = [(24, 40), (64, 40), (104, 32)], [(8, 16), (136, 16)]
 DIAGONAL = [(32, 32), (64, 32), (96, 32)], [(8, 24), (128, 24)]
 FIRST = [(40, 40), (80, 40)], [(8, 32), (120, 32)]
@@ -35,8 +35,9 @@
 
 def kernel(
     design, solid, void, load_in, support_in, eta_in, weight_in, out,
-    raw, masks, fb, lt, ls, ring, lr, sr, inm, inv, tw, hh, cond, zz, idg, ww, kk, rowp, rowz, ee, turned_e,
-    in_sem, send_f, recv_f, send_e, recv_e, send_m, recv_m, send_t, recv_t,
+    raw, masks, fb, rim_out, rim_in, lt, ls, ring, lr, sr, inm, inv, tw, hh, cond, zz, idg, ww, kk, rowp, rowz, ee, turned_e,
+    eta_held, weight_held,
+    in_sem, mask_sem, send_f, recv_f, send_e, recv_e, send_m, recv_m, send_t, recv_t,
     send_p, recv_p, send_z, recv_z,
 ):
     me = lax.axis_index("space")
@@ -60,14 +61,22 @@
         for j, step in enumerate((-1, 0, 1)):
             lane = pl.multiple_of(slabs[step] * THICK, THICK)
             loads.append(
-                pltpu.make_async_copy(source.at[:, :, pl.ds(lane, THICK)], masks.at[2 + 3 * i + j], in_sem.at[3 + 3 * i + j])
+                pltpu.make_async_copy(source.at[:, :, pl.ds(lane, THICK)], masks.at[2 + 3 * i + j], mask_sem.at[0])
             )
+    loads.append(pltpu.make_async_copy(eta_in, eta_held, in_sem.at[3]))
+    loads.append(pltpu.make_async_copy(weight_in, weight_held, in_sem.at[4]))
+    mask_loads = pltpu.make_async_copy(masks.at[pl.ds(2, 6)], masks.at[pl.ds(2, 6)], mask_sem.at[0])
     for item in loads[:3]:
         item.start()
 
     near = (1, -1, 2, -2)
     halo = [(slabs[e], space_at(d)) for d in near[::-1] + (0,) for e in (1, -1)]
     halo += [(slab, space_at(d)) for d in near]
+    barrier = pltpu.get_barrier_semaphore()
+    for place in halo:
+        pl.semaphore_signal(barrier, inc=1, device_id=place, device_id_type=MESH)
+    for item in loads[9:]:
+        item.start()
     rows_y = [(me + (dy << 5)) & 0xE0 for dy in range(NYC)]
     rows_x = [(me + (dx << 3)) & 0x18 for dx in range(NXC)]
     low = me & 0x07
@@ -85,12 +94,9 @@
         z = jnp.where(z >= NZC, z - NZC, z)
         levels.append((z >> 2, base + ((z & 3) << 1)))
     stack = [(levels[dz][0], levels[dz][1] + cores[dc]) for dz, dc in stack]
-    partners = halo + plane + stack
-
-    barrier = pltpu.get_barrier_semaphore()
-    for place in partners:
+    for place in plane + stack:
         pl.semaphore_signal(barrier, inc=1, device_id=place, device_id_type=MESH)
-    for item in loads[3:]:
+    for item in loads[3:9]:
         item.start()
 
     lane = lax.broadcasted_iota(jnp.int32, (1, 128), 1)
@@ -108,14 +114,18 @@
     def swap(v):
         return pltpu.roll(v, WIDTH, 1)
 
-    eta = eta_in[0].astype(F32) / 1000.0
-    row = lax.broadcasted_iota(jnp.int32, (8, 128), 0)
-    tw[slab] = jnp.where(row == 0, eta, weight_in[0])
-
     for item in loads[:3]:
         item.wait()
-    fixed = jnp.where(masks[0] == 1, 1.0, jnp.where(masks[1] == 1, 0.0, raw[...]))
-    fb[2, LO:HI, :] = fixed.reshape(128, 128).T
+    fixed = jnp.where(masks[0] == 1, 1.0, jnp.where(masks[1] == 1, 0.0, raw[...])).reshape(128, 128).T
+    fb[2, LO:HI, :] = fixed
+    rim_out[0] = fixed[THICK - REACH :, :]
+    rim_out[1] = fixed[:REACH, :]
+
+    for item in loads[9:]:
+        item.wait()
+    eta = eta_held[0, 0].astype(F32) / 1000.0
+    row = lax.broadcasted_iota(jnp.int32, (8, 128), 0)
+    tw[slab] = jnp.where(row == 0, eta, weight_held[0, 0])
 
     def remote(source, target, ssem, rsem, place):
         return pltpu.make_async_remote_copy(
@@ -125,7 +135,7 @@
     def main_copy(i, source, target, step):
         return remote(
             fb.at[source, pl.ds(LO, THICK), :], fb.at[target, pl.ds(LO, THICK), :],
-            send_f.at[i], recv_f.at[i], (slab, space_at(step)),
+            send_f.at[0], recv_f.at[i], (slab, space_at(step)),
         )
 
     from_outer = main_copy(0, 2, 2 + inward, -inward)
@@ -133,17 +143,11 @@
     from_partner = main_copy(2, 2, 2 - inward, inward)
     relay = main_copy(3, 2 - inward, 2 - 2 * inward, inward)
     rims, marks, small = [], [], []
-    for i, d in enumerate(near[::-1] + (0,)):
+    for d in near[::-1] + (0,):
         for j, e in enumerate((1, -1)):
-            src, dst = (HI - 8, LO - 8) if e == 1 else (LO, HI)
-            rims.append(
-                remote(
-                    fb.at[2, pl.ds(src, 8), :], fb.at[2 - d, pl.ds(dst, 8), :],
-                    send_e.at[2 * i + j], recv_e.at[2 * i + j], (slabs[e], space_at(d)),
-                )
-            )
+            rims.append(remote(rim_out.at[j], rim_in.at[2 - d, j], send_e.at[0], recv_e.at[0], (slabs[e], space_at(d))))
     for i, e in enumerate((1, -1)):
-        small.append(remote(tw.at[slab], tw.at[slab], send_t.at[i], recv_t.at[i], (slabs[e], me)))
+        small.append(remote(tw.at[slab], tw.at[slab], send_t.at[0], recv_t.at[0], (slabs[e], me)))
 
     spill_up = ((me & 7) == 7).astype(jnp.int32)
     spill_down = ((me & 7) == 0).astype(jnp.int32)
@@ -153,16 +157,23 @@
         marks.append(
             remote(
                 lt.at[:, pl.ds(start, THICK + 16), :], ls.at[i, :, pl.ds(LO - 8, THICK + 16), :],
-                send_m.at[i], recv_m.at[i], (place, space_at(d)),
+                send_m.at[0], recv_m.at[0], (place, space_at(d)),
             )
         )
 
-    pl.semaphore_wait(barrier, len(partners))
+    def whole(ref, ssem, rsem):
+        return remote(ref, ref, ssem.at[0], rsem.at[0], (slab, space_at(1)))
+
+    all_main = whole(fb.at[pl.ds(0, 4), pl.ds(LO, THICK), :], send_f, recv_f)
+    all_rims = whole(rim_in, send_e, recv_e)
+    all_marks = whole(ls.at[:, :, pl.ds(LO - 8, THICK + 16), :], send_m, recv_m)
+    all_small = whole(tw.at[pl.ds(0, 2)], send_t, recv_t)
+
+    pl.semaphore_wait(barrier, len(halo) + len(plane) + len(stack))
     for item in rims[:8] + [from_outer, from_far, from_partner] + rims[8:] + small:
         item.start()
 
-    for item in loads[3:]:
-        item.wait()
+    mask_loads.wait()
     for i in range(2):
         for j in range(3):
             turned = masks[2 + 3 * i + j].reshape(128, 128).astype(F32).T
@@ -192,21 +203,20 @@
 
     from_outer.wait_recv()
     relay.start()
-    for item in [from_partner, from_far] + small:
+    for item in (from_partner, from_far, all_small, relay):
         item.wait_recv()
-    relay.wait_recv()
-
-    def form_rings(chunks):
-        for r0, n in chunks:
-            rows = slice(r0, r0 + n)
-            ring[0, rows, :] = fb[2, rows, :] * inm[0, rows, :]
-            p1, m1, p2, m2 = fb[3, rows, :], fb[1, rows, :], fb[4, rows, :], fb[0, rows, :]
-            ring[1, rows, :] = swap(jnp.where(upper, m1, p1)) * inm[1, rows, :]
-            ring[2, rows, :] = jnp.where(upper, p1, m1) * inm[2, rows, :]
-            ring[3, rows, :] = swap(jnp.where(upper, m2, p2)) * inm[3, rows, :]
-            ring[4, rows, :] = jnp.where(upper, p2, m2) * inm[4, rows, :]
-
-    form_rings(OWN)
+
+    def form_rings(r0, n, bricks):
+        rows = slice(r0, r0 + n)
+        m2, m1, own, p1, p2 = bricks
+        ring[0, rows, :] = own * inm[0, rows, :]
+        ring[1, rows, :] = swap(jnp.where(upper, m1, p1)) * inm[1, rows, :]
+        ring[2, rows, :] = jnp.where(upper, p1, m1) * inm[2, rows, :]
+        ring[3, rows, :] = swap(jnp.where(upper, m2, p2)) * inm[3, rows, :]
+        ring[4, rows, :] = jnp.where(upper, p2, m2) * inm[4, rows, :]
+
+    for r0, n in OWN:
+        form_rings(r0, n, [fb[i, r0 : r0 + n, :] for i in range(5)])
 
     etas, tops, scales, weights = [], [], [], []
     for g in range(NPROJ):
@@ -315,8 +325,7 @@
 
     project(FILTER[0])
 
-    for item in marks:
-        item.wait_recv()
+    all_marks.wait_recv()
 
     for r0, n in ALL:
         rows = slice(r0, r0 + n)
@@ -337,9 +346,9 @@
     first_step(FIRST[0])
     second_step(SECOND[0])
 
-    for item in rims:
-        item.wait_recv()
-    form_rings(RIM)
+    all_rims.wait_recv()
+    for j, r0 in enumerate((LO - REACH, HI)):
+        form_rings(r0, REACH, [rim_in[i, j] for i in range(5)])
     project(FILTER[1])
     precondition(DIAGONAL[1])
     first_step(FIRST[1])
@@ -366,7 +375,7 @@
         return terms[0]
 
     in_plane = share(line, rowp, send_p, recv_p, plane)
-    for item in [from_outer, from_far, from_partner, relay] + rims + small + marks:
+    for item in (all_main, all_rims, all_small, all_marks):
         item.wait_send()
 
     for g in range(NPROJ):
@@ -419,12 +428,14 @@
     return pl.pallas_call(
         kernel,
         out_shape=pltpu.VMEM((DEPTH, WIDTH, THICK), F32),
-        in_specs=[pl.BlockSpec(memory_space=pl.ANY)] * 5 + [pl.BlockSpec(memory_space=pltpu.SMEM)] * 2,
+        in_specs=[pl.BlockSpec(memory_space=pl.ANY)] * 5 + [pl.BlockSpec(memory_space=pltpu.HBM)] * 2,
         out_specs=pl.BlockSpec(memory_space=pltpu.VMEM),
         scratch_shapes=[
             pltpu.VMEM((DEPTH, WIDTH, THICK), F32),
             pltpu.VMEM((8, DEPTH, WIDTH, THICK), jnp.int32),
             pltpu.VMEM((5, ROWS, 128), F32),
+            pltpu.VMEM((2, REACH, 128), F32),
+            pltpu.VMEM((5, 2, REACH, 128), F32),
             pltpu.VMEM((2, 3 * THICK + 16, 128), F32),
             pltpu.VMEM((2, 2, ROWS, 128), F32),
             pltpu.VMEM((5, ROWS, 128), F32),
@@ -443,16 +454,21 @@
             pltpu.VMEM((NZC * NCORE, 1, 128), F32),
             pltpu.VMEM((NPROJ, 3, THICK, 128), F32),
             pltpu.VMEM((NPROJ, 3, THICK, 128), F32),
-            dma((9,)),
-            dma((4,)), dma((4,)),
-            dma((10,)), dma((10,)),
-            dma((2,)), dma((2,)),
-            dma((2,)), dma((2,)),
+            pltpu.SMEM((1, 1), jnp.int32),
+            pltpu.SMEM((1, 1), F32),
+            dma((5,)), dma((1,)),
+            dma((1,)), dma((4,)),
+            dma((1,)), dma((1,)),
+            dma((1,)), dma((1,)),
+            dma((1,)), dma((1,)),
             dma((1,)), dma((1,)),
             dma((1,)), dma((1,)),
         ],
         compiler_params=pltpu.CompilerParams(collective_id=0, has_side_effects=True),
-    )(design, solid_mask, void_mask, load_mask, support_mask, thresholds, group_weight)
+    )(
+        design, solid_mask, void_mask, load_mask, support_mask,
+        thresholds.reshape(1, 1), group_weight.reshape(1, 1),
+    )
 
 
 def solution(mesh):

time: 45.6 us -> 44.9 us (0.985)
  Pallas kernels: 43.4 us -> 42.8 us
    pallas_call x1, Pallas kernels: 43.4 us -> 42.8 us  [local(): pl.pallas_call(kernel, out_shape=pltpu.VMEM((DEPTH, WIDTH, THICK), F32),...]
where the time goes in v4:
time: 44.9 us; the launch traced here: 44.8 us
  Pallas kernels  42.8 us (95%)
  between operations  1.3 us (3%)
  local copies, waits for them, and re-layouts  0.63 us (1%)
    pallas_call x1, Pallas kernels, local(): pl.pallas_call(kernel, out_shape=pltpu.VMEM((DEPTH, WIDTH, THICK), F32),...  42.8 us

profile of v4, /device:TPU:1, one launch (start us, length us, event | category | flops | bytes accessed | tf_op | source)
XLA Modules:
  0.0 44.8 jit_solution(3784221159652053249)
XLA Ops:
  1.3 42.8 %shard_map.73 = f32[2,64,128]{2,1,0:T(8,128)S(1)} custom-call(f32[2,64,128]{2,1,0:T(8,128)} %design.1, s32[2,64,128]{2,1,0:T(8,128)} %solid.1, s32[2,64,128]{2,1,0:T(8,128)} %void.1, s32[2,64,384]{2,1,0:T(8,128)} %load_in.1, s32[2,64,384]{2,1,0:T(8,128)} %support_in.1, s32[1,1]{1,0:T(1,128)} %bitcast.2.eta_in, f32[1,1]{1,0:T(1,128)} %bitcast.3.weight_in), custom_call_target="tpu_custom_call" | custom-call | tf_op jit(solution)/shard_map/pallas_call | solution.py:428
  44.1 0.6 %copy.9 = f32[2,64,128]{2,1,0:T(8,128)} copy(f32[2,64,128]{2,1,0:T(8,128)S(1)} %shard_map.73) | data formatting | bytes 131072

commit v5 on v4

--- a/solution.py
+++ b/solution.py
@@ -170,7 +170,7 @@
     all_small = whole(tw.at[pl.ds(0, 2)], send_t, recv_t)
 
     pl.semaphore_wait(barrier, len(halo) + len(plane) + len(stack))
-    for item in rims[:8] + [from_outer, from_far, from_partner] + rims[8:] + small:
+    for item in rims[:8] + [from_outer, from_partner] + rims[8:] + small:
         item.start()
 
     mask_loads.wait()
@@ -182,8 +182,6 @@
                 lt[i, 8 + 3 * THICK :, :] = turned[:8, :]
             if j == 2:
                 lt[i, 0:8, :] = turned[120:, :]
-    for item in marks:
-        item.start()
 
     count_y = has_up.astype(F32) + has_down.astype(F32)
     for k in range(5):
@@ -201,6 +199,9 @@
                 total = total + EDGE * (count_x * (count_y + count_z) + pair) + CORNER * (count_x * pair)
                 inv[k, r0 : r0 + n, :] = BETA / total
 
+    from_far.start()
+    for item in marks:
+        item.start()
     from_outer.wait_recv()
     relay.start()
     for item in (from_partner, from_far, all_small, relay):
@@ -231,19 +232,15 @@
     def project(chunks):
         for r0, n in chunks:
             rows = slice(r0, r0 + n)
-            centre, side = [], []
-            for k in range(5):
-                v = ring[k, rows, :]
-                zb = ring[k, r0 + 1 : r0 + n + 1, :] + ring[k, r0 - 1 : r0 + n - 1, :]
-                yb = y_up(v) + y_down(v)
-                cross = y_up(zb) + y_down(zb)
-                faces = zb + yb
-                if k < 4:
-                    centre.append(2.0 * v + faces + EDGE * cross)
-                side.append(v + EDGE * faces + CORNER * cross)
+            plain = [ring[k, rows, :] for k in range(5)]
+            beside = [ring[k, r0 + 1 : r0 + n + 1, :] + ring[k, r0 - 1 : r0 + n - 1, :] for k in range(5)]
             for k in range(4):
-                inner = side[k - 1] if k else swap(side[0])
-                f8 = (centre[k] + (inner + side[k + 1])) * inv[k, rows, :]
+                v, zb = plain[k], beside[k]
+                vx = (plain[k - 1] if k else swap(v)) + plain[k + 1]
+                zx = (beside[k - 1] if k else swap(zb)) + beside[k + 1]
+                line_y = v + EDGE * (zb + vx) + CORNER * zx
+                total = 2.0 * v + (zb + vx) + EDGE * zx + (y_up(line_y) + y_down(line_y))
+                f8 = total * inv[k, rows, :]
                 mask = inm[k, rows, :]
                 for g in range(NPROJ):
                     t = jnp.tanh(f8 - etas[g])
@@ -260,19 +257,22 @@
                     rows = slice(r0, r0 + n)
                     h = hh[g, k, rows, :]
                     inner = hh[g, k - 1, rows, :] if k else swap(h)
-                    links = [
-                        h + inner,
-                        h + hh[g, k + 1, rows, :],
-                        h + y_up(h),
-                        h + y_down(h),
-                        h + hh[g, k, r0 + 1 : r0 + n + 1, :],
-                        h + hh[g, k, r0 - 1 : r0 + n - 1, :],
+                    near_h = [
+                        inner,
+                        hh[g, k + 1, rows, :],
+                        y_up(h),
+                        y_down(h),
+                        hh[g, k, r0 + 1 : r0 + n + 1, :],
+                        hh[g, k, r0 - 1 : r0 + n - 1, :],
                     ]
                     diag = sr[k, rows, :]
-                    for i, link in enumerate(links):
-                        diag = diag + link
+                    if k == 2:
+                        diag = diag + 6.0 * h
+                    for i, other in enumerate(near_h):
                         if k < 2:
-                            cond[g, k, i, rows, :] = link
+                            other = h + other
+                            cond[g, k, i, rows, :] = other
+                        diag = diag + other
                     inverse = inm[k, rows, :] / diag
                     zz[g, k, rows, :] = lr[k, rows, :] * inverse
                     if k < 2:

time: 44.9 us -> 44.9 us (level)
  no operation moved by 1% of the time
where the time goes in v5:
time: 44.9 us; the launch traced here: 44.7 us
  Pallas kernels  42.7 us (95%)
  between operations  1.3 us (3%)
  local copies, waits for them, and re-layouts  0.63 us (1%)
    pallas_call x1, Pallas kernels, local(): pl.pallas_call(kernel, out_shape=pltpu.VMEM((DEPTH, WIDTH, THICK), F32),...  42.7 us

profile of v5, /device:TPU:1, one launch (start us, length us, event | category | flops | bytes accessed | tf_op | source)
XLA Modules:
  0.0 44.7 jit_solution(11011478691166371861)
XLA Ops:
  1.3 42.7 %shard_map.73 = f32[2,64,128]{2,1,0:T(8,128)S(1)} custom-call(f32[2,64,128]{2,1,0:T(8,128)} %design.1, s32[2,64,128]{2,1,0:T(8,128)} %solid.1, s32[2,64,128]{2,1,0:T(8,128)} %void.1, s32[2,64,384]{2,1,0:T(8,128)} %load_in.1, s32[2,64,384]{2,1,0:T(8,128)} %support_in.1, s32[1,1]{1,0:T(1,128)} %bitcast.2.eta_in, f32[1,1]{1,0:T(1,128)} %bitcast.3.weight_in), custom_call_target="tpu_custom_call" | custom-call | tf_op jit(solution)/shard_map/pallas_call | solution.py:428
  44.0 0.6 %copy.9 = f32[2,64,128]{2,1,0:T(8,128)} copy(f32[2,64,128]{2,1,0:T(8,128)S(1)} %shard_map.73) | data formatting | bytes 131072

commit v6 on v5

--- a/solution.py
+++ b/solution.py
@@ -27,10 +27,10 @@
 OWN = [(LO + i, 32) for i in range(0, THICK, 32)]
 ALL = [(LO - 8, 8)] + OWN + [(HI, 8)]
 REACH = 4
-FILTER = [(24, 40), (64, 40), (104, 32)], [(8, 16), (136, 16)]
-DIAGONAL = [(32, 32), (64, 32), (96, 32)], [(8, 24), (128, 24)]
-FIRST = [(40, 40), (80, 40)], [(8, 32), (120, 32)]
-SECOND = [(48, 32), (80, 32)], [(16, 32), (112, 32)]
+FILTER = [(24, 16), (40, 16), (56, 16), (72, 16), (88, 16), (104, 16), (120, 16)], [(8, 16), (136, 16)]
+DIAGONAL = [(32, 16), (48, 16), (64, 16), (80, 16), (96, 16), (112, 16)], [(8, 16), (24, 8), (128, 16), (144, 8)]
+FIRST = [(40, 16), (56, 16), (72, 16), (88, 16), (104, 16)], [(8, 16), (24, 16), (120, 16), (136, 16)]
+SECOND = [(48, 16), (64, 16), (80, 16), (96, 16)], [(16, 16), (32, 16), (112, 16), (128, 16)]
 
 
 def kernel(
@@ -81,11 +81,12 @@
     rows_x = [(me + (dx << 3)) & 0x18 for dx in range(NXC)]
     low = me & 0x07
     plane = sorted(
-        ((dy, dx) for dy in range(NYC) for dx in range(NXC) if dy or dx),
+        ((dy, dx, dc) for dy in range(NYC) for dx in range(NXC) for dc in range(NCORE) if dy or dx or dc),
         key=lambda p: -(min(p[0], NYC - p[0]) + min(p[1], NXC - p[1])),
     )
-    plane = [(slab, rows_y[dy] + rows_x[dx] + low) for dy, dx in plane]
-    stack = sorted(((dz, dc) for dz in range(NZC) for dc in range(NCORE) if dz or dc), key=lambda p: -min(p[0], NZC - p[0]))
+    lows = (low, low + inward)
+    plane = [(slab, rows_y[dy] + rows_x[dx] + lows[dc]) for dy, dx, dc in plane]
+    stack = sorted(((dz, dc) for dz in range(NZC) for dc in range(1) if dz), key=lambda p: -min(p[0], NZC - p[0]))
     base = me & 0xF8
     cores = (core, 1 - core)
     levels = []
@@ -393,10 +394,10 @@
             turned_e[g, i] = ee[g, i].T
 
     in_plane.wait_recv()
-    in_stack = share(gathered(rowp, NXC * NYC), rowz, send_z, recv_z, stack)
+    in_stack = share(gathered(rowp, NXC * NYC * NCORE), rowz, send_z, recv_z, stack)
     in_plane.wait_send()
     in_stack.wait_recv()
-    line = gathered(rowz, NZC * NCORE)
+    line = gathered(rowz, NZC)
 
     rz0, pq1 = line, pltpu.roll(line, 96, 1)
     qdq, wsw = pltpu.roll(line, 64, 1), pltpu.roll(line, 32, 1)
@@ -450,8 +451,8 @@
             pltpu.VMEM((NPROJ, 2, ROWS, 128), F32),
             pltpu.VMEM((NPROJ, 2, ROWS, 128), F32),
             pltpu.VMEM((NPROJ, ROWS, 128), F32),
-            pltpu.VMEM((NXC * NYC, 1, 128), F32),
-            pltpu.VMEM((NZC * NCORE, 1, 128), F32),
+            pltpu.VMEM((NXC * NYC * NCORE, 1, 128), F32),
+            pltpu.VMEM((NZC, 1, 128), F32),
             pltpu.VMEM((NPROJ, 3, THICK, 128), F32),
             pltpu.VMEM((NPROJ, 3, THICK, 128), F32),
             pltpu.SMEM((1, 1), jnp.int32),

time: 44.9 us -> 43.9 us (0.978)
  Pallas kernels: 42.7 us -> 41.8 us
    pallas_call x1, Pallas kernels: 42.7 us -> 41.8 us  [local(): pl.pallas_call(kernel, out_shape=pltpu.VMEM((DEPTH, WIDTH, THICK), F32),...]
where the time goes in v6:
time: 43.9 us; the launch traced here: 43.8 us
  Pallas kernels  41.8 us (95%)
  between operations  1.3 us (3%)
  local copies, waits for them, and re-layouts  0.63 us (1%)
    pallas_call x1, Pallas kernels, local(): pl.pallas_call(kernel, out_shape=pltpu.VMEM((DEPTH, WIDTH, THICK), F32),...  41.8 us

profile of v6, /device:TPU:1, one launch (start us, length us, event | category | flops | bytes accessed | tf_op | source)
XLA Modules:
  0.0 43.8 jit_solution(1389161241140565463)
XLA Ops:
  1.3 41.8 %shard_map.73 = f32[2,64,128]{2,1,0:T(8,128)S(1)} custom-call(f32[2,64,128]{2,1,0:T(8,128)} %design.1, s32[2,64,128]{2,1,0:T(8,128)} %solid.1, s32[2,64,128]{2,1,0:T(8,128)} %void.1, s32[2,64,384]{2,1,0:T(8,128)} %load_in.1, s32[2,64,384]{2,1,0:T(8,128)} %support_in.1, s32[1,1]{1,0:T(1,128)} %bitcast.2.eta_in, f32[1,1]{1,0:T(1,128)} %bitcast.3.weight_in), custom_call_target="tpu_custom_call" | custom-call | tf_op jit(solution)/shard_map/pallas_call | solution.py:429
  43.1 0.6 %copy.9 = f32[2,64,128]{2,1,0:T(8,128)} copy(f32[2,64,128]{2,1,0:T(8,128)S(1)} %shard_map.73) | data formatting | bytes 131072

commit v7 on v5

--- a/solution.py
+++ b/solution.py
@@ -27,10 +27,10 @@
 OWN = [(LO + i, 32) for i in range(0, THICK, 32)]
 ALL = [(LO - 8, 8)] + OWN + [(HI, 8)]
 REACH = 4
-FILTER = [(24, 40), (64, 40), (104, 32)], [(8, 16), (136, 16)]
-DIAGONAL = [(32, 32), (64, 32), (96, 32)], [(8, 24), (128, 24)]
-FIRST = [(40, 40), (80, 40)], [(8, 32), (120, 32)]
-SECOND = [(48, 32), (80, 32)], [(16, 32), (112, 32)]
+FILTER = [(24, 16), (40, 16), (56, 16), (72, 16), (88, 16), (104, 16), (120, 16)], [(8, 16), (136, 16)]
+DIAGONAL = [(32, 16), (48, 16), (64, 16), (80, 16), (96, 16), (112, 16)], [(8, 16), (24, 8), (128, 16), (144, 8)]
+FIRST = [(40, 16), (56, 16), (72, 16), (88, 16), (104, 16)], [(8, 16), (24, 16), (120, 16), (136, 16)]
+SECOND = [(48, 16), (64, 16), (80, 16), (96, 16)], [(16, 16), (32, 16), (112, 16), (128, 16)]
 
 
 def kernel(
@@ -374,7 +374,7 @@
             terms = [a + b for a, b in zip(terms[::2], terms[1::2])] + terms[len(terms) // 2 * 2 :]
         return terms[0]
 
-    in_plane = share(line, rowp, send_p, recv_p, plane)
+    in_plane = share(line, rowz, send_z, recv_z, stack)
     for item in (all_main, all_rims, all_small, all_marks):
         item.wait_send()
 
@@ -393,10 +393,10 @@
             turned_e[g, i] = ee[g, i].T
 
     in_plane.wait_recv()
-    in_stack = share(gathered(rowp, NXC * NYC), rowz, send_z, recv_z, stack)
+    in_stack = share(gathered(rowz, NZC * NCORE), rowp, send_p, recv_p, plane)
     in_plane.wait_send()
     in_stack.wait_recv()
-    line = gathered(rowz, NZC * NCORE)
+    line = gathered(rowp, NXC * NYC)
 
     rz0, pq1 = line, pltpu.roll(line, 96, 1)
     qdq, wsw = pltpu.roll(line, 64, 1), pltpu.roll(line, 32, 1)

time: 44.9 us -> 43.9 us (0.978)
  Pallas kernels: 42.7 us -> 41.8 us
    pallas_call x1, Pallas kernels: 42.7 us -> 41.8 us  [local(): pl.pallas_call(kernel, out_shape=pltpu.VMEM((DEPTH, WIDTH, THICK), F32),...]
where the time goes in v7:
time: 43.9 us; the launch traced here: 43.7 us
  Pallas kernels  41.8 us (95%)
  between operations  1.3 us (3%)
  local copies, waits for them, and re-layouts  0.63 us (1%)
    pallas_call x1, Pallas kernels, local(): pl.pallas_call(kernel, out_shape=pltpu.VMEM((DEPTH, WIDTH, THICK), F32),...  41.8 us

profile of v7, /device:TPU:1, one launch (start us, length us, event | category | flops | bytes accessed | tf_op | source)
XLA Modules:
  0.0 43.7 jit_solution(6320916738006429187)
XLA Ops:
  1.3 41.8 %shard_map.73 = f32[2,64,128]{2,1,0:T(8,128)S(1)} custom-call(f32[2,64,128]{2,1,0:T(8,128)} %design.1, s32[2,64,128]{2,1,0:T(8,128)} %solid.1, s32[2,64,128]{2,1,0:T(8,128)} %void.1, s32[2,64,384]{2,1,0:T(8,128)} %load_in.1, s32[2,64,384]{2,1,0:T(8,128)} %support_in.1, s32[1,1]{1,0:T(1,128)} %bitcast.2.eta_in, f32[1,1]{1,0:T(1,128)} %bitcast.3.weight_in), custom_call_target="tpu_custom_call" | custom-call | tf_op jit(solution)/shard_map/pallas_call | solution.py:428
  43.1 0.6 %copy.9 = f32[2,64,128]{2,1,0:T(8,128)} copy(f32[2,64,128]{2,1,0:T(8,128)S(1)} %shard_map.73) | data formatting | bytes 131072
